TPU v7x, 128 devices: a whole 4x4x4 slice. The times are simulated.
128 devices in a mesh: lag: 16 (over z_lo, x, core), row: 8 (over y, z_hi).
Axes of the slice: x: 4, y: 4, z: 4 (z_hi: 2, z_lo: 2; z = z_hi * 2 + z_lo), core: 2. Of those that a mesh axis runs over, the one named last changes fastest.
Arguments:
- lag_matrix: bfloat16 [16, 8192, 8192], P('lag', 'row'), may hold values from -0.015625 to 0.015625
- past_current: bfloat16 [16, 256, 8192], P('lag', None, 'row'), may hold values from -6 to 6
- excitation: float32 [2, 256, 8192], P(None, None, 'row'), may hold values from -6 to 6
- block_inverse: float32 [64, 128, 128], P('row'), may hold values from -2 to 3
Outputs:
- currents: bfloat16 [2, 256, 8192], P(None, 'lag', 'row')
All inputs are finite; a program needn't handle non-finite values.
Results may differ from a plain program's by a relative error of at most 0.002.
Values may be sent and summed in bfloat16 or wider, within the bound.
A program may use at most 64 MiB of HBM per device.

v0:
```python
import jax
import jax.numpy as jnp
from jax import lax
from jax.sharding import PartitionSpec as P

STEPS = 2


def in_blocks(x, dim, peers):
    before, after = (x.shape[:dim], x.shape[dim + 1 :])
    return jnp.moveaxis(x.reshape(*before, peers, -1, *after), dim, 0)


def summed_on_arrival(x, axis, dim):
    tiles = in_blocks(x, dim, lax.axis_size(axis))
    arrived = lax.all_to_all(tiles, axis, split_axis=0, concat_axis=0, tiled=True)
    return arrived.sum(axis=0)


def in_order(tiles, dim):
    tiles = jnp.moveaxis(tiles, 0, dim)
    lengths = tiles.shape
    return tiles.reshape(*lengths[:dim], lengths[dim] * lengths[dim + 1], *lengths[dim + 2 :])


def from_everyone(x, axis):
    peers = lax.axis_size(axis)
    return lax.all_to_all(jnp.broadcast_to(x[None], (peers, *x.shape)), axis, 0, 0, tiled=True)


def gather_directly(x, axis, dim):
    return in_order(from_everyone(x, axis), dim)


def from_behind(x, axis, by):
    peers = lax.axis_size(axis)
    pairs = [(i, i + by) for i in range(peers) if 0 <= i + by < peers]
    return lax.ppermute(x, axis, pairs)


def solve_blocks(source, block_inverse):
    count = source.shape[0]
    pieces = source.reshape(count, block_inverse.shape[0], block_inverse.shape[1])
    result = jnp.einsum("bij,rbj->rbi", block_inverse, pieces, precision=lax.Precision.HIGHEST)
    return result.reshape(count, source.shape[1]).astype(jnp.bfloat16)


def advance(older, newest, leading):
    incoming_rest = jnp.concatenate([older, leading[:-1]], axis=0)
    first = lax.axis_index("lag") == 0
    head = jnp.where(first, newest[None], incoming_rest)
    return jnp.concatenate([head, incoming_rest[1:]], axis=0)


def per_device(lag_matrix, past_current, excitation, block_inverse):
    lag_count = lax.axis_size("lag")
    excite_all = past_current.shape[1]
    share = excite_all // lag_count
    offset = lax.axis_index("lag") * share
    current_loc = past_current
    results = []
    for step in range(STEPS):
        partial_value = jnp.einsum(
            "lrc,lkc->rk",
            lax.all_gather(current_loc, "row", axis=2, tiled=True),
            lag_matrix,
            preferred_element_type=jnp.float32,
        )
        history = summed_on_arrival(partial_value, "lag", 0)
        mine = lax.dynamic_slice_in_dim(excitation[step], offset, share, 0)
        newest_part = solve_blocks(mine - history, block_inverse)
        results.append(newest_part)
        if step + 1 < STEPS:
            newest = gather_directly(newest_part, "lag", 0)
        if step + 1 < STEPS:
            older = from_behind(current_loc, "lag", 1)
            current_loc = advance(older, newest, current_loc)
    return jnp.stack(results)


def solution(mesh):
    in_specs = (
        P("lag", "row", None),
        P("lag", None, "row"),
        P(None, None, "row"),
        P("row", None, None),
    )
    out_specs = P(None, "lag", "row")
    return jax.shard_map(
        per_device, mesh=mesh, in_specs=in_specs, out_specs=out_specs, check_vma=False
    )
```

profile of v0, /device:TPU:1, one launch (start us, length us, event | category | flops | bytes accessed | tf_op | source)
XLA Modules:
  0.0 246.1 jit_solution(4965949983607384674)
XLA Ops:
  6.5 0.0 copy-start
  6.5 0.0 all-gather.3.cloned.1.call-start
  6.5 0.7 all-gather.3.cloned.1.call-update
  7.3 76.9 %all-gather.3.cloned.1.call-done = bf16[1,256,8192]{2,1,0:T(8,128)(2,1)} async-done(((bf16[1,256,1024]{2,1,0:T(8,128)(2,1)}), bf16[1,256,8192]{2,1,0:T(8,128)(2,1)}) %all-gather.3.cloned.1.call-update) | async-done | bytes 4194320 | tf_op jit(solution)/shard_map/all_gather | solution.py:65
  84.2 0.0 copy-start.1
  84.2 12.6 %fusion.2 = f32[16,16,1024]{2,1,0:T(8,128)} fusion(bf16[16,16,8192]{2,1,0:T(8,128)(2,1)} %bitcast.44, bf16[1,1024,8192]{2,1,0:T(8,128)(2,1)} %param.4), kind=kOutput, calls=%fused_computation.2 | convolution fusion | flops 4294967296 | bytes 22020096 | tf_op jit(solution)/shard_map/lrc,lkc->rk/dot_general | solution.py:63
  96.7 5.4 %all-to-all-start = ((f32[16,16,1024]{2,1,0:T(8,128)}), f32[16,16,1024]{2,1,0:T(8,128)S(1)}, u32[]{:S(2)}, u32[]{:S(2)}) async-start(f32[16,16,1024]{2,1,0:T(8,128)} %fusion.2), calls=%async_computation | async-start | bytes 2097152 | tf_op jit(solution)/shard_map/all_to_all | solution.py:16
  102.2 0.0 copy-done.1
  102.2 3.5 %collective-permute-start = (bf16[1,256,1024]{2,1,0:T(8,128)(2,1)S(1)}, bf16[1,256,1024]{2,1,0:T(8,128)(2,1)}, u32[]{:S(2)}, u32[]{:S(2)}) collective-permute-start(bf16[1,256,1024]{2,1,0:T(8,128)(2,1)S(1)} %copy-done.1), channel_id=1, source_target_pairs={{0,8},{8,16},{16,24},{24,32},{32,40},{40,48},{48,56},{56,64},{64,7... | collective-permute-start | bytes 1572872 | tf_op jit(solution)/shard_map/ppermute | solution.py:38
  105.7 1.7 fusion.7
  107.5 10.6 %all-to-all-done = f32[16,16,1024]{2,1,0:T(8,128)S(1)} async-done(((f32[16,16,1024]{2,1,0:T(8,128)}), f32[16,16,1024]{2,1,0:T(8,128)S(1)}, u32[]{:S(2)}, u32[]{:S(2)}) %all-to-all-start) | async-done | bytes 1048608 | tf_op jit(solution)/shard_map/all_to_all | solution.py:16
  118.0 0.1 reduce_sum.22
  118.1 0.0 copy-done
  118.1 0.9 convolution_convert_fusion.1
  119.0 0.9 broadcast_in_dim.2
  119.9 4.1 %all-to-all-start.1 = ((bf16[16,16,1024]{2,1,0:T(8,128)(2,1)}), bf16[16,16,1024]{2,1,0:T(8,128)(2,1)S(1)}, u32[]{:S(2)}, u32[]{:S(2)}) async-start(bf16[16,16,1024]{2,1,0:T(8,128)(2,1)} %broadcast_in_dim.2), calls=%async_computation.1 | async-start | bytes 1048576 | tf_op jit(solution)/shard_map/all_to_all | solution.py:28
  124.0 0.0 all-gather.5.cloned.1.call-start
  124.0 0.0 collective-permute-done
  124.0 9.9 %all-to-all-done.1 = bf16[16,16,1024]{2,1,0:T(8,128)(2,1)S(1)} async-done(((bf16[16,16,1024]{2,1,0:T(8,128)(2,1)}), bf16[16,16,1024]{2,1,0:T(8,128)(2,1)S(1)}, u32[]{:S(2)}, u32[]{:S(2)}) %all-to-all-start.1) | async-done | bytes 524320 | tf_op jit(solution)/shard_map/all_to_all | solution.py:28
  134.0 1.9 bitcast_select_fusion
  135.9 0.0 all-gather.5.cloned.1.call-update
  135.9 67.8 %all-gather.5.cloned.1.call-done = bf16[1,256,8192]{2,1,0:T(8,128)(2,1)} async-done(((bf16[1,256,1024]{2,1,0:T(8,128)(2,1)}), bf16[1,256,8192]{2,1,0:T(8,128)(2,1)}) %all-gather.5.cloned.1.call-update) | async-done | bytes 4194320 | tf_op jit(solution)/shard_map/all_gather | solution.py:65
  203.7 12.5 %fusion = f32[16,16,1024]{2,1,0:T(8,128)} fusion(bf16[16,16,8192]{2,1,0:T(8,128)(2,1)} %bitcast.43, bf16[1,1024,8192]{2,1,0:T(8,128)(2,1)} %param.4), kind=kOutput, calls=%fused_computation | convolution fusion | flops 4294967296 | bytes 22020096 | tf_op jit(solution)/shard_map/lrc,lkc->rk/dot_general | solution.py:63
  216.2 5.4 %all-to-all-start.2 = ((f32[16,16,1024]{2,1,0:T(8,128)}), f32[16,16,1024]{2,1,0:T(8,128)S(1)}, u32[]{:S(2)}, u32[]{:S(2)}) async-start(f32[16,16,1024]{2,1,0:T(8,128)} %fusion), calls=%async_computation.2 | async-start | bytes 2097152 | tf_op jit(solution)/shard_map/all_to_all | solution.py:16
  221.7 15.8 %all-to-all-done.2 = f32[16,16,1024]{2,1,0:T(8,128)S(1)} async-done(((f32[16,16,1024]{2,1,0:T(8,128)}), f32[16,16,1024]{2,1,0:T(8,128)S(1)}, u32[]{:S(2)}, u32[]{:S(2)}) %all-to-all-start.2) | async-done | bytes 1048608 | tf_op jit(solution)/shard_map/all_to_all | solution.py:16
  237.5 0.1 reduce_sum.24
  237.6 0.9 fusion.4
  238.6 0.6 pad_maximum_fusion
  (13 shorter events, 0.2 us)
Async XLA Ops:
  6.5 111.6 %copy-start = (f32[8,128,128]{2,1,0:T(8,128)S(1)}, f32[8,128,128]{2,1,0:T(8,128)}, u32[]{:S(2)}) copy-start(f32[8,128,128]{2,1,0:T(8,128)} %param.7) | copy-start | bytes 1572868
  6.5 77.6 %all-gather.3.cloned.1.call-start = ((), (), s32[]{:S(2)}) async-start(), calls=%async_computation.3 | async-start | bytes 4718592 | tf_op jit(solution)/shard_map/all_gather | solution.py:65
  84.2 18.0 %copy-start.1 = (bf16[1,256,1024]{2,1,0:T(8,128)(2,1)S(1)}, bf16[1,256,1024]{2,1,0:T(8,128)(2,1)}, u32[]{:S(2)}) copy-start(bf16[1,256,1024]{2,1,0:T(8,128)(2,1)} %param.5) | copy-start | bytes 1572868
  96.7 21.3 %all-to-all-start = ((f32[16,16,1024]{2,1,0:T(8,128)}), f32[16,16,1024]{2,1,0:T(8,128)S(1)}, u32[]{:S(2)}, u32[]{:S(2)}) async-start(f32[16,16,1024]{2,1,0:T(8,128)} %fusion.2), calls=%async_computation | async-start | bytes 2097152 | tf_op jit(solution)/shard_map/all_to_all | solution.py:16
  102.2 21.9 %collective-permute-start = (bf16[1,256,1024]{2,1,0:T(8,128)(2,1)S(1)}, bf16[1,256,1024]{2,1,0:T(8,128)(2,1)}, u32[]{:S(2)}, u32[]{:S(2)}) collective-permute-start(bf16[1,256,1024]{2,1,0:T(8,128)(2,1)S(1)} %copy-done.1), channel_id=1, source_target_pairs={{0,8},{8,16},{16,24},{24,32},{32,40},{40,48},{48,56},{56,64},{64,7... | collective-permute-start | bytes 1572872 | tf_op jit(solution)/shard_map/ppermute | solution.py:38
  119.9 14.1 %all-to-all-start.1 = ((bf16[16,16,1024]{2,1,0:T(8,128)(2,1)}), bf16[16,16,1024]{2,1,0:T(8,128)(2,1)S(1)}, u32[]{:S(2)}, u32[]{:S(2)}) async-start(bf16[16,16,1024]{2,1,0:T(8,128)(2,1)} %broadcast_in_dim.2), calls=%async_computation.1 | async-start | bytes 1048576 | tf_op jit(solution)/shard_map/all_to_all | solution.py:28
  124.0 79.7 %all-gather.5.cloned.1.call-start = ((), (), s32[]{:S(2)}) async-start(), calls=%async_computation.4 | async-start | bytes 4718592 | tf_op jit(solution)/shard_map/all_gather | solution.py:65
  216.2 21.3 %all-to-all-start.2 = ((f32[16,16,1024]{2,1,0:T(8,128)}), f32[16,16,1024]{2,1,0:T(8,128)S(1)}, u32[]{:S(2)}, u32[]{:S(2)}) async-start(f32[16,16,1024]{2,1,0:T(8,128)} %fusion), calls=%async_computation.2 | async-start | bytes 2097152 | tf_op jit(solution)/shard_map/all_to_all | solution.py:16
Sparse Core Ops, SparseCore 0:
  9.7 74.3 all-gather.2
  136.0 67.6 all-gather.4
where the time goes:
time: 247 us; the launch traced here: 246 us
  waiting for transfers between devices  182 us (74%)
  matrix products  26.9 us (11%)
  starting transfers between devices  18.5 us (7%)
  between operations  13.5 us (5%)
  local copies, waits for them, and re-layouts  2.71 us (1%)
  other arithmetic  2.68 us (1%)
    all_gather x2, waiting for transfers between devices, per_device(): lax.all_gather(current_loc, 'row', axis=2, tiled=True)  145 us
    all_to_all x2, waiting for transfers between devices, summed_on_arrival(): lax.all_to_all(tiles, axis, split_axis=0, concat_axis=0, tiled=True)  26.3 us
    dot_general x2, matrix products, per_device(): jnp.einsum('lrc,lkc->rk', lax.all_gather(current_loc, 'row', axis=2, tile...  25.1 us
    all_to_all x2, starting transfers between devices, summed_on_arrival(): lax.all_to_all(tiles, axis, split_axis=0, concat_axis=0, tiled=True)  10.9 us
    all_to_all x1, waiting for transfers between devices, from_everyone(): lax.all_to_all(jnp.broadcast_to(x[None], (peers, *x.shape)), axis, 0, 0,...  9.92 us
  transfers between devices with their start and end apart: 6, of which 5 were waited for; matrix products, arithmetic and copies ran while one was open for 1% of the time, Pallas kernels for 0%

commit v1 on v0

v1 whole, which is shorter than its diff:
```python
import jax
import jax.numpy as jnp
from jax import lax
from jax.experimental import pallas as pl
from jax.experimental.pallas import tpu as pltpu
from jax.sharding import PartitionSpec as P

MESH = pl.DeviceIdType.MESH
NT = (((1,), (1,)), ((), ()))
F32 = jnp.float32


def kernel(m_hbm, p_hbm, e_hbm, b_hbm, out_ref, mv, g, tg, acc, acc2, xbuf, part, rbuf, ex, binv, newest,
           m_sem, loc_sem, ga_s, ga_r, gt_s, gt_r, sib_s, sib_r, sh_s, sh_r, x_s, x_r, rs_s, rs_r, nb_s, nb_r):
    lag, row = lax.axis_index("lag"), lax.axis_index("row")
    core, x, zl = lag % 2, (lag // 2) % 4, lag // 8
    y, h = row // 2, row % 2
    yp, ym, y2, ho = (y + 1) % 4, (y + 3) % 4, (y + 2) % 4, 1 - h
    E, W = p_hbm.shape[1], p_hbm.shape[2]
    S = ex.shape[1]
    rows = {"0": (0, E // 2), "0a": (0, E // 4), "0b": (E // 4, E // 4),
            "1": (E // 2, E // 2), "1a": (E // 2, E // 4), "1b": (3 * E // 4, E // 4)}

    def lag_of(x_, zl_, c_):
        return (zl_ * 4 + x_) * 2 + c_

    def slot(y_, h_):
        return y_ * 2 + h_

    barrier = pltpu.get_barrier_semaphore()
    for peer in (slot(yp, h), slot(ym, h), slot(y, ho)):
        pl.semaphore_signal(barrier, 1, device_id={"row": peer}, device_id_type=MESH)
    for k in range(1, 16):
        pl.semaphore_signal(barrier, 1, device_id={"lag": (lag + k) % 16}, device_id_type=MESH)

    order = [(y, h), (ym, h), (yp, h), (y, ho), (y2, h), (ym, ho), (yp, ho), (y2, ho)]
    loads = [pltpu.make_async_copy(p_hbm.at[0], g.at[row], loc_sem.at[0]),
             pltpu.make_async_copy(e_hbm.at[:, pl.ds(pl.multiple_of(lag * S, S), S)], ex, loc_sem.at[1]),
             pltpu.make_async_copy(b_hbm, binv, loc_sem.at[2])]
    loads[0].start()
    m_loads = []
    for k, (y_, h_) in enumerate(order):
        s = slot(y_, h_)
        m_loads.append(pltpu.make_async_copy(m_hbm.at[0, :, pl.ds(pl.multiple_of(s * W, W), W)], mv.at[s], m_sem.at[k]))
        m_loads[-1].start()
    loads[1].start()
    loads[2].start()
    pl.semaphore_wait(barrier, 18)

    def mm(dst, src, s, first):
        @pl.loop(0, 4)
        def _(n):
            cols = pl.ds(pl.multiple_of(n * (W // 4), W // 4), W // 4)
            v = lax.dot_general(src[s], mv[s, cols, :], NT, preferred_element_type=F32)
            if first:
                dst[:, cols] = v
            else:
                dst[:, cols] += v

    def gather(buf, own, ss, rs, on_shard):
        zp, to_p, to_m = slot(y, ho), slot(yp, h), slot(ym, h)
        sends = [((y, h), "0", to_p), ((y, h), "0", to_m), ((ym, h), "0a", to_p), ((yp, h), "0b", to_m),
                 ((y, h), "0", zp), ((ym, h), "0", zp), ((yp, h), "0", zp), ((y2, h), "0a", zp), ((y2, h), "0b", zp),
                 ((y, h), "1", to_p), ((y, h), "1", to_m), ((ym, h), "1a", to_p), ((yp, h), "1b", to_m),
                 ((y, h), "1", zp), ((y, ho), "1", to_p), ((y, ho), "1", to_m), ((ym, ho), "1a", to_p), ((yp, ho), "1b", to_m)]
        arrivals = [((ym, h), "0"), ((yp, h), "0"), ((y2, h), "0a"), ((y2, h), "0b"),
                    ((y, ho), "0"), ((ym, ho), "0"), ((yp, ho), "0"), ((y2, ho), "0a"), ((y2, ho), "0b"),
                    ((ym, h), "1"), ((yp, h), "1"), ((y2, h), "1a"), ((y2, h), "1b"),
                    ((y, ho), "1"), ((ym, ho), "1"), ((yp, ho), "1"), ((y2, ho), "1a"), ((y2, ho), "1b")]
        started = []

        def start(*which):
            for i in which:
                (y_, h_), rr, to = sends[i]
                lo, n = rows[rr]
                s = slot(y_, h_)
                src = own.at[pl.ds(lo, n)] if i in (0, 1, 4, 9, 10, 13) else buf.at[s, pl.ds(lo, n)]
                cp = pltpu.make_async_remote_copy(src, buf.at[s, pl.ds(lo, n)], ss.at[i], rs.at[i],
                                                  device_id={"row": to}, device_id_type=MESH)
                cp.start()
                started.append(cp)

        def wait(*which):
            for i in which:
                (y_, h_), rr = arrivals[i]
                lo, n = rows[rr]
                s = slot(y_, h_)
                ref = buf.at[s, pl.ds(lo, n)]
                pltpu.make_async_remote_copy(ref, ref, ss.at[i], rs.at[i], device_id={"row": sends[i][2]},
                                             device_id_type=MESH).wait_recv()

        start(13, 0, 1, 9, 10, 4)
        on_shard(0)
        yield
        wait(13)
        start(14, 15)
        wait(0)
        start(2, 5)
        wait(1)
        start(3, 6)
        wait(9)
        start(11)
        on_shard(1)
        wait(10)
        start(12)
        on_shard(2)
        yield
        wait(4)
        on_shard(3)
        wait(2)
        start(7)
        wait(3)
        start(8)
        wait(14)
        start(16)
        wait(15)
        start(17)
        yield
        wait(11, 12)
        on_shard(4)
        wait(5)
        on_shard(5)
        wait(6)
        on_shard(6)
        wait(7, 8, 16, 17)
        on_shard(7)
        for cp in started:
            cp.wait_send()

    def sibling_copy(s, k):
        return pltpu.make_async_remote_copy(g.at[s], tg.at[s], sib_s.at[k], sib_r.at[k],
                                            device_id={"lag": lag + 1 - 2 * core}, device_id_type=MESH)

    shift = pltpu.make_async_remote_copy(p_hbm.at[0], tg.at[row], sh_s.at[0], sh_r.at[0],
                                         device_id={"lag": (lag + 1) % 16}, device_id_type=MESH)

    def a_shard(k):
        s = slot(*order[k])
        if k == 0:
            loads[0].wait()

        @pl.when(core == 0)
        def _():
            sibling_copy(s, k).start()
        m_loads[k].wait()
        mm(acc, g, s, k == 0)

    stages = gather(g, p_hbm.at[0], ga_s, ga_r, a_shard)
    next(stages)

    @pl.when((core == 1) & (lag < 15))
    def _():
        shift.start()
    for _ in stages:
        pass

    def reduce_and_solve(step, total, between):
        chips = [(dx, dz) for dx in (1, 3, 2, 0) for dz in (0, 1)]
        chips = [c for c in chips if c != (0, 0)] + [(0, 0)]

        def rows_of(k, c_):
            dx, dz = chips[k]
            return pl.ds(pl.multiple_of(lag_of((x + dx) % 4, (zl + dz) % 2, c_) * S, S), S)

        pair = []
        for k in range(8):
            cp = pltpu.make_async_remote_copy(total.at[rows_of(k, 1 - core)], xbuf.at[step, k], x_s.at[step, k], x_r.at[step, k],
                                              device_id={"lag": lag + 1 - 2 * core}, device_id_type=MESH)
            cp.start()
            pair.append(cp)
        sent = []
        for k in range(8):
            pair[k].wait_recv()
            part[step, k] = total[rows_of(k, core), :] + xbuf[step, k]
            if k < 7:
                dx, dz = chips[k]
                cp = pltpu.make_async_remote_copy(part.at[step, k], rbuf.at[step, k], rs_s.at[step, k], rs_r.at[step, k],
                                                  device_id={"lag": lag_of((x + dx) % 4, (zl + dz) % 2, core)}, device_id_type=MESH)
                cp.start()
                sent.append(cp)
        between()
        history = part[step, 7]
        for k in range(7):
            sent[k].wait_recv()
            history = history + rbuf[step, k]
        source = ex[step] - history
        for b in range(binv.shape[0]):
            cols = pl.ds(b * 128, 128)
            v = lax.dot_general(source[:, b * 128:(b + 1) * 128], binv[b], NT, precision=lax.Precision.HIGHEST,
                                preferred_element_type=F32)
            newest[:, cols] = v.astype(newest.dtype)
        out_ref[step] = newest[...]
        return pair + sent

    older = (core == 0) & (lag > 0)

    def t_shard(k):
        if k in (2, 3, 4, 7):
            return

    t_stages = gather(tg, tg.at[row], gt_s, gt_r, lambda k: None)

    loads[1].wait()
    loads[2].wait()
    sends = reduce_and_solve(0, acc, lambda: None)

    mine = pl.ds(pl.multiple_of(lag * S, S), S)
    to_first = pltpu.make_async_remote_copy(newest, tg.at[row, mine], nb_s.at[0], nb_r.at[lag],
                                            device_id={"lag": 0}, device_id_type=MESH)

    @pl.when(lag > 0)
    def _():
        to_first.start()

    @pl.when(older)
    def _():
        shift.wait_recv()
        for _ in gather(tg, tg.at[row], gt_s, gt_r, lambda k: None):
            pass

        @pl.loop(0, 8)
        def _(s):
            @pl.when(s == 0)
            def _():
                mm(acc2, tg, s, True)

            @pl.when(s > 0)
            def _():
                mm(acc2, tg, s, False)

    @pl.when(core == 1)
    def _():
        for k in range(8):
            s = slot(*order[k])
            sibling_copy(s, k).wait_recv()
            mm(acc2, tg, s, k == 0)

    @pl.when(lag == 0)
    def _():
        tg[row, mine, :] = newest[...]
        for l in range(1, 16):
            ref = tg.at[row, pl.ds(l * S, S)]
            pltpu.make_async_remote_copy(ref, ref, nb_s.at[0], nb_r.at[l], device_id={"lag": l}, device_id_type=MESH).wait_recv()
        for _ in gather(tg, tg.at[row], gt_s, gt_r, lambda k: mm(acc2, tg, slot(*order[k]), k == 0)):
            pass

    @pl.when(lag > 0)
    def _():
        to_first.wait_send()
    sends += reduce_and_solve(1, acc2, lambda: None)

    for cp in sends:
        cp.wait_send()

    @pl.when(core == 0)
    def _():
        for k in range(8):
            sibling_copy(slot(*order[k]), k).wait_send()

    @pl.when((core == 1) & (lag < 15))
    def _():
        shift.wait_send()


def per_device(lag_matrix, past_current, excitation, block_inverse):
    E, W = past_current.shape[1:]
    S = E // 16
    nb = block_inverse.shape[0]
    bf = past_current.dtype
    dma = pltpu.SemaphoreType.DMA
    return pl.pallas_call(
        kernel,
        out_shape=jax.ShapeDtypeStruct((2, S, W), bf),
        in_specs=[pl.BlockSpec(memory_space=pl.ANY)] * 4,
        out_specs=pl.BlockSpec(memory_space=pltpu.VMEM),
        scratch_shapes=[
            pltpu.VMEM((8, W, W), bf), pltpu.VMEM((8, E, W), bf), pltpu.VMEM((8, E, W), bf),
            pltpu.VMEM((E, W), F32), pltpu.VMEM((E, W), F32),
            pltpu.VMEM((2, 8, S, W), F32), pltpu.VMEM((2, 8, S, W), F32), pltpu.VMEM((2, 7, S, W), F32),
            pltpu.VMEM((2, S, W), F32), pltpu.VMEM((nb, 128, 128), F32), pltpu.VMEM((S, W), bf),
            dma((8,)), dma((3,)), dma((18,)), dma((18,)), dma((18,)), dma((18,)), dma((8,)), dma((8,)), dma((1,)), dma((1,)),
            dma((2, 8)), dma((2, 8)), dma((2, 7)), dma((2, 7)), dma((1,)), dma((16,)),
        ],
        compiler_params=pltpu.CompilerParams(collective_id=0, has_side_effects=True, vmem_limit_bytes=60 << 20),
    )(lag_matrix, past_current, excitation, block_inverse)


def solution(mesh):
    in_specs = (P("lag", "row", None), P("lag", None, "row"), P(None, None, "row"), P("row", None, None))
    return jax.shard_map(per_device, mesh=mesh, in_specs=in_specs, out_specs=P(None, "lag", "row"), check_vma=False)
```

time: 247 us -> 104 us (0.42)
  waiting for transfers between devices: 182 us -> 0 us
  Pallas kernels: 0 us -> 103 us
  matrix products: 26.9 us -> 0 us
  starting transfers between devices: 18.5 us -> 0 us
  between operations: 13.5 us -> 0.01 us
  other arithmetic: 2.68 us -> 0 us
    all_gather x2 -> x0, waiting for transfers between devices: 145 us -> none  [per_device(): lax.all_gather(current_loc, 'row', axis=2, tiled=True)]
    pallas_call x0 -> x1, Pallas kernels: none -> 103 us  [per_device(): pl.pallas_call(kernel, out_shape=jax.ShapeDtypeStruct((2, S, W), bf), in_...]
    all_to_all x3 -> x0, waiting for transfers between devices: 36.3 us -> none  [the longest x2 26.3 us: summed_on_arrival(): lax.all_to_all(tiles, axis, split_axis=0, concat_axis=0, tiled=True)]
    dot_general x4 -> x0, matrix products: 26.9 us -> none  [the longest x2 25.1 us: per_device(): jnp.einsum('lrc,lkc->rk', lax.all_gather(current_loc, 'row', axis=2, tile...]
    all_to_all x3 -> x0, starting transfers between devices: 15 us -> none  [the longest x2 10.9 us: summed_on_arrival(): lax.all_to_all(tiles, axis, split_axis=0, concat_axis=0, tiled=True)]
    ppermute x1 -> x0, starting transfers between devices: 3.54 us -> none  [from_behind(): return lax.ppermute(x, axis, pairs)]
  transfers between devices with their start and end apart: 6 -> 0, of which waited for: 5 -> 0; matrix products, arithmetic and copies ran while one was open for 1% -> 0% of each run, Pallas kernels for 0% -> 0%
where the time goes in v1:
time: 104 us
  Pallas kernels  103 us (99%)
  local copies, waits for them, and re-layouts  1.47 us (1%)
    pallas_call x1, Pallas kernels, per_device(): pl.pallas_call(kernel, out_shape=jax.ShapeDtypeStruct((2, S, W), bf), in_...  103 us

profile of v1, /device:TPU:1, one launch (start us, length us, event | category | flops | bytes accessed | tf_op | source)
XLA Modules:
  0.0 104.2 jit_solution(15121880537168661881)
XLA Ops:
  0.0 102.8 %shard_map.46 = bf16[2,16,1024]{2,1,0:T(8,128)(2,1)} custom-call(bf16[1,1024,8192]{2,1,0:T(8,128)(2,1)} %m_hbm.1, bf16[1,256,1024]{2,1,0:T(8,128)(2,1)} %p_hbm.1, f32[2,256,1024]{2,1,0:T(8,128)} %e_hbm.1, f32[8,128,128]{2,1,0:T(8,128)} %b_hbm.1), custom_call_target="tpu_custom_call" | custom-call | tf_op jit(solution)/shard_map/pallas_call | solution.py:271
  102.8 1.5 %copy.6 = bf16[2,16,1024]{2,1,0:T(8,128)(2,1)} copy(bf16[2,16,1024]{2,1,0:T(8,128)(2,1)} %shard_map.46) | data formatting | bytes 131072

commit v2 on v0

v2 whole, which is shorter than its diff:
```python
import jax
import jax.numpy as jnp
from jax import lax
from jax.experimental import pallas as pl
from jax.experimental.pallas import tpu as pltpu
from jax.sharding import PartitionSpec as P

MESH = pl.DeviceIdType.MESH
NT = (((1,), (1,)), ((), ()))
F32 = jnp.float32
CHIPS = [(1, 0), (1, 1), (3, 0), (3, 1), (2, 0), (2, 1), (0, 1), (0, 0)]


def kernel(m_hbm, p_hbm, e_hbm, b_hbm, out_ref, mv, g, tg, acc, acc2, xbuf, part, rbuf, ex, binv, newest,
           m_sem, loc_sem, ga_s, ga_r, gt_s, gt_r, sib_s, sib_r, sh_s, sh_r, x_s, x_r, rs_s, rs_r, nb_s, nb_r):
    lag, row = lax.axis_index("lag"), lax.axis_index("row")
    core, x, zl = lag % 2, (lag // 2) % 4, lag // 8
    chip = lag // 2
    y, h = row // 2, row % 2
    yp, ym, y2, ho = (y + 1) % 4, (y + 3) % 4, (y + 2) % 4, 1 - h
    W = p_hbm.shape[-1]
    S = ex.shape[1]
    older = (core == 0) & (lag > 0)

    shards = [y * 2 + h, ym * 2 + h, yp * 2 + h, y * 2 + ho, y2 * 2 + h, ym * 2 + ho, yp * 2 + ho, y2 * 2 + ho]
    sibling = lag + 1 - 2 * core
    elder = (lag + 1) % 16
    peers = [(((zl + dz) % 2) * 4 + (x + dx) % 4) for dx, dz in CHIPS]
    peer_lags = [p * 2 + core for p in peers]

    barrier = pltpu.get_barrier_semaphore()
    for k in (1, 2, 3):
        pl.semaphore_signal(barrier, 1, device_id={"row": shards[k]}, device_id_type=MESH)
    for k in range(1, 16):
        pl.semaphore_signal(barrier, 1, device_id={"lag": (lag + k) % 16}, device_id_type=MESH)

    loads = [pltpu.make_async_copy(p_hbm.at[:, c], g.at[c, row], loc_sem.at[c]) for c in range(2)]
    loads += [pltpu.make_async_copy(e_hbm.at[:, pl.ds(pl.multiple_of(lag * S, S), S)], ex, loc_sem.at[2]),
              pltpu.make_async_copy(b_hbm, binv, loc_sem.at[3])]
    m_loads = [pltpu.make_async_copy(m_hbm.at[0, :, pl.ds(pl.multiple_of(s * W, W), W)], mv.at[s], m_sem.at[k])
               for k, s in enumerate(shards)]
    for cp in loads[:2] + m_loads + loads[2:]:
        cp.start()
    loads[0].wait()
    loads[1].wait()
    pl.semaphore_wait(barrier, 18)

    def mm(dst, src, s, first):
        v_rows = src.shape[1] * src.shape[2]

        @pl.loop(0, 4)
        def _(n):
            cols = pl.ds(pl.multiple_of(n * (W // 4), W // 4), W // 4)
            v = lax.dot_general(src[s].reshape(v_rows, W), mv[s, cols, :], NT, preferred_element_type=F32)
            v = v.reshape(src.shape[1], src.shape[2], W // 4)
            if first:
                dst[:, :, cols] = v
            else:
                dst[:, :, cols] += v

    class Gather:
        SENDS = [(0, "0", 2), (0, "0", 1), (1, "0a", 2), (2, "0b", 1), (0, "0", 3), (1, "0", 3), (2, "0", 3), (4, "0a", 3),
                 (4, "0b", 3), (0, "1", 2), (0, "1", 1), (1, "1a", 2), (2, "1b", 1), (0, "1", 3), (3, "1", 2), (3, "1", 1),
                 (5, "1a", 2), (6, "1b", 1)]
        ARRIVE = [(1, "0"), (2, "0"), (4, "0a"), (4, "0b"), (3, "0"), (5, "0"), (6, "0"), (7, "0a"), (7, "0b"), (1, "1"),
                  (2, "1"), (4, "1a"), (4, "1b"), (3, "1"), (5, "1"), (6, "1"), (7, "1a"), (7, "1b")]

        def __init__(self, buf, c, ss, rs, split):
            self.buf, self.c, self.ss, self.rs = buf, c, ss, rs
            a, n = split // 2, 8 - split
            self.blocks = {"0": (0, split), "0a": (0, a), "0b": (a, split - a),
                           "1": (split, n), "1a": (split, n // 2), "1b": (split + n // 2, n - n // 2)}

        def copy(self, i, k, blocks, to):
            lo, n = self.blocks[blocks]
            ref = self.buf.at[self.c, shards[k], pl.ds(lo, n)]
            return pltpu.make_async_remote_copy(ref, ref, self.ss.at[self.c, i], self.rs.at[self.c, i],
                                                device_id={"row": shards[to]}, device_id_type=MESH)

        def start(self, *which):
            for i in which:
                self.copy(i, *self.SENDS[i]).start()

        def wait(self, *which):
            for i in which:
                k, blocks = self.ARRIVE[i]
                self.copy(i, k, blocks, self.SENDS[i][2]).wait_recv()

        def drain(self):
            for i in range(18):
                self.copy(i, *self.SENDS[i]).wait_send()

        def own(self):
            self.start(13, 0, 1, 9, 10, 4)

        def relay1(self, on_shard):
            self.wait(13)
            self.start(14, 15)
            self.wait(0)
            self.start(2, 5)
            self.wait(1)
            self.start(3, 6)
            self.wait(9)
            self.start(11)
            on_shard(1)
            self.wait(10)
            self.start(12)
            on_shard(2)

        def relay2(self, on_shard):
            self.wait(4)
            on_shard(3)
            self.wait(2)
            self.start(7)
            self.wait(3)
            self.start(8)
            self.wait(14)
            self.start(16)
            self.wait(15)
            self.start(17)

        def rest(self, on_shard):
            self.wait(11, 12)
            on_shard(4)
            self.wait(5)
            on_shard(5)
            self.wait(6)
            on_shard(6)
            self.wait(7, 8, 16, 17)
            on_shard(7)

    def sibling_copy(c, k):
        s = shards[k]
        return pltpu.make_async_remote_copy(g.at[c, s], tg.at[c, s], sib_s.at[c, k], sib_r.at[c, k],
                                            device_id={"lag": sibling}, device_id_type=MESH)

    shift = [pltpu.make_async_remote_copy(g.at[c, row], tg.at[c, row], sh_s.at[c], sh_r.at[c],
                                          device_id={"lag": elder}, device_id_type=MESH) for c in range(2)]

    def exchange(step, total, c, k):
        return pltpu.make_async_remote_copy(total.at[c, peers[k]], xbuf.at[step, k], x_s.at[step, k], x_r.at[step, k],
                                            device_id={"lag": sibling}, device_id_type=MESH)

    def to_owner(step, k):
        return pltpu.make_async_remote_copy(part.at[step, k], rbuf.at[step, k], rs_s.at[step, k], rs_r.at[step, k],
                                            device_id={"lag": peer_lags[k]}, device_id_type=MESH)

    def hand_over(step, total, c):
        for k in range(8):
            exchange(step, total, c, k).start()

    def reduce_send(step, total, c):
        for k in range(8):
            exchange(step, total, c, k).wait_recv()
            part[step, k] = total[c, peers[k]] + xbuf[step, k]
            if k < 7:
                to_owner(step, k).start()

    def finish(step):
        history = part[step, 7]
        for k in range(7):
            to_owner(step, k).wait_recv()
            history = history + rbuf[step, k]
        source = ex[step] - history
        for b in range(binv.shape[0]):
            v = lax.dot_general(source[:, b * 128:(b + 1) * 128], binv[b], NT, precision=lax.Precision.HIGHEST,
                                preferred_element_type=F32)
            newest[step, :, pl.ds(b * 128, 128)] = v.astype(newest.dtype)
        out_ref[step] = newest[step]

    def to_first(c):
        return pltpu.make_async_remote_copy(newest.at[0], tg.at[c, row, chip], nb_s.at[0], nb_r.at[lag],
                                            device_id={"lag": 0}, device_id_type=MESH)

    def from_lag(c, k):
        ref = tg.at[c, row, k]
        return pltpu.make_async_remote_copy(ref, ref, nb_s.at[0], nb_r.at[2 * k + c], device_id={"lag": 0}, device_id_type=MESH)

    def a_shard(c):
        def on_shard(k):
            @pl.when(core == 0)
            def _():
                sibling_copy(c, k).start()
            if c == 0:
                m_loads[k].wait()
            mm(acc.at[c], g.at[c], shards[k], k == 0)
        return on_shard

    def t_shard(c):
        return lambda k: mm(acc2.at[c], tg.at[c], shards[k], k == 0)

    a = [Gather(g, c, ga_s, ga_r, 4 - c) for c in range(2)]
    t = [Gather(tg, c, gt_s, gt_r, 4 - c) for c in range(2)]

    a[0].own()

    @pl.when((core == 1) & (lag < 15))
    def _():
        shift[0].start()
        shift[1].start()
    a_shard(0)(0)
    a[0].relay1(a_shard(0))
    a[1].own()
    a[0].relay2(a_shard(0))
    a_shard(1)(0)
    a[0].rest(a_shard(0))

    @pl.when(core == 1)
    def _():
        hand_over(0, acc, 0)

    @pl.when(core == 0)
    def _():
        reduce_send(0, acc, 0)
    a[1].relay1(a_shard(1))
    a[1].relay2(a_shard(1))
    loads[2].wait()
    loads[3].wait()

    @pl.when(core == 0)
    def _():
        finish(0)

    @pl.when(lag == 0)
    def _():
        tg[0, row, 0] = newest[0]

    @pl.when(older)
    def _():
        to_first(0).start()
        shift[0].wait_recv()
        shift[1].wait_recv()
        t[0].own()
    a[1].rest(a_shard(1))

    @pl.when(core == 0)
    def _():
        hand_over(0, acc, 1)

    @pl.when(core == 1)
    def _():
        reduce_send(0, acc, 1)
        for k in range(8):
            sibling_copy(0, k).wait_recv()
            t_shard(0)(k)
        hand_over(1, acc2, 0)
        finish(0)
        to_first(1).start()
        for k in range(8):
            sibling_copy(1, k).wait_recv()
            t_shard(1)(k)
        reduce_send(1, acc2, 1)

    @pl.when(older)
    def _():
        t_shard(0)(0)
        t[0].relay1(t_shard(0))
        t[1].own()
        t[0].relay2(t_shard(0))
        t_shard(1)(0)
        t[0].rest(t_shard(0))
        reduce_send(1, acc2, 0)
        t[1].relay1(t_shard(1))
        t[1].relay2(t_shard(1))
        t[1].rest(t_shard(1))
        hand_over(1, acc2, 1)

    @pl.when(lag == 0)
    def _():
        for k in range(1, 8):
            from_lag(0, k).wait_recv()
        t[0].own()
        t_shard(0)(0)
        t[0].relay1(t_shard(0))
        t[0].relay2(t_shard(0))
        t[0].rest(t_shard(0))
        reduce_send(1, acc2, 0)
        for k in range(8):
            from_lag(1, k).wait_recv()
        t[1].own()
        t_shard(1)(0)
        t[1].relay1(t_shard(1))
        t[1].relay2(t_shard(1))
        t[1].rest(t_shard(1))
        hand_over(1, acc2, 1)

    finish(1)

    a[0].drain()
    a[1].drain()
    for k in range(7):
        to_owner(0, k).wait_send()
        to_owner(1, k).wait_send()

    @pl.when(core == 0)
    def _():
        t[0].drain()
        t[1].drain()
        for k in range(8):
            for c in range(2):
                sibling_copy(c, k).wait_send()
                exchange(c, (acc, acc2)[c], 1, k).wait_send()

    @pl.when(lag > 0)
    def _():
        to_first(0).wait_send()

    @pl.when(core == 1)
    def _():
        for k in range(8):
            for step in range(2):
                exchange(step, (acc, acc2)[step], 0, k).wait_send()

    @pl.when((core == 1) & (lag < 15))
    def _():
        shift[0].wait_send()
        shift[1].wait_send()


def per_device(lag_matrix, past_current, excitation, block_inverse):
    E, W = past_current.shape[1:]
    S = E // 16
    nb = block_inverse.shape[0]
    bf = past_current.dtype
    dma = pltpu.SemaphoreType.DMA
    past = past_current.reshape(8, 2, S, W)
    return pl.pallas_call(
        kernel,
        out_shape=jax.ShapeDtypeStruct((2, S, W), bf),
        in_specs=[pl.BlockSpec(memory_space=pl.ANY)] * 4,
        out_specs=pl.BlockSpec(memory_space=pltpu.VMEM),
        scratch_shapes=[
            pltpu.VMEM((8, W, W), bf), pltpu.VMEM((2, 8, 8, S, W), bf), pltpu.VMEM((2, 8, 8, S, W), bf),
            pltpu.VMEM((2, 8, S, W), F32), pltpu.VMEM((2, 8, S, W), F32),
            pltpu.VMEM((2, 8, S, W), F32), pltpu.VMEM((2, 8, S, W), F32), pltpu.VMEM((2, 7, S, W), F32),
            pltpu.VMEM((2, S, W), F32), pltpu.VMEM((nb, 128, 128), F32), pltpu.VMEM((2, S, W), bf),
            dma((8,)), dma((4,)), dma((2, 18)), dma((2, 18)), dma((2, 18)), dma((2, 18)), dma((2, 8)), dma((2, 8)),
            dma((2,)), dma((2,)), dma((2, 8)), dma((2, 8)), dma((2, 7)), dma((2, 7)), dma((1,)), dma((16,)),
        ],
        compiler_params=pltpu.CompilerParams(collective_id=0, has_side_effects=True, vmem_limit_bytes=60 << 20),
    )(lag_matrix, past, excitation, block_inverse)


def solution(mesh):
    in_specs = (P("lag", "row", None), P("lag", None, "row"), P(None, None, "row"), P("row", None, None))
    return jax.shard_map(per_device, mesh=mesh, in_specs=in_specs, out_specs=P(None, "lag", "row"), check_vma=False)
```

time: 247 us -> 95.8 us (0.39)
  waiting for transfers between devices: 182 us -> 0 us
  Pallas kernels: 0 us -> 93.7 us
  matrix products: 26.9 us -> 0 us
  starting transfers between devices: 18.5 us -> 0 us
  between operations: 13.5 us -> 0.01 us
  other arithmetic: 2.68 us -> 0 us
    all_gather x2 -> x0, waiting for transfers between devices: 145 us -> none  [per_device(): lax.all_gather(current_loc, 'row', axis=2, tiled=True)]
    pallas_call x0 -> x1, Pallas kernels: none -> 93.7 us  [per_device(): pl.pallas_call(kernel, out_shape=jax.ShapeDtypeStruct((2, S, W), bf), in_...]
    all_to_all x3 -> x0, waiting for transfers between devices: 36.3 us -> none  [the longest x2 26.3 us: summed_on_arrival(): lax.all_to_all(tiles, axis, split_axis=0, concat_axis=0, tiled=True)]
    dot_general x4 -> x0, matrix products: 26.9 us -> none  [the longest x2 25.1 us: per_device(): jnp.einsum('lrc,lkc->rk', lax.all_gather(current_loc, 'row', axis=2, tile...]
    all_to_all x3 -> x0, starting transfers between devices: 15 us -> none  [the longest x2 10.9 us: summed_on_arrival(): lax.all_to_all(tiles, axis, split_axis=0, concat_axis=0, tiled=True)]
    ppermute x1 -> x0, starting transfers between devices: 3.54 us -> none  [from_behind(): return lax.ppermute(x, axis, pairs)]
  transfers between devices with their start and end apart: 6 -> 0, of which waited for: 5 -> 0; matrix products, arithmetic and copies ran while one was open for 1% -> 0% of each run, Pallas kernels for 0% -> 0%
where the time goes in v2:
time: 95.8 us; the launch traced here: 95.2 us
  Pallas kernels  93.7 us (98%)
  local copies, waits for them, and re-layouts  1.47 us (2%)
    pallas_call x1, Pallas kernels, per_device(): pl.pallas_call(kernel, out_shape=jax.ShapeDtypeStruct((2, S, W), bf), in_...  93.7 us

profile of v2, /device:TPU:1, one launch (start us, length us, event | category | flops | bytes accessed | tf_op | source)
XLA Modules:
  0.0 95.2 jit_solution(2697688141394141601)
XLA Ops:
  0.0 93.7 %shard_map.46 = bf16[2,16,1024]{2,1,0:T(8,128)(2,1)} custom-call(bf16[1,1024,8192]{2,1,0:T(8,128)(2,1)} %m_hbm.1, bf16[8,2,16,1024]{3,2,1,0:T(8,128)(2,1)} %bitcast.1, f32[2,256,1024]{2,1,0:T(8,128)} %e_hbm.1, f32[8,128,128]{2,1,0:T(8,128)} %b_hbm.1), custom_call_target="tpu_custom_call" | custom-call | tf_op jit(solution)/shard_map/pallas_call | solution.py:327
  93.7 1.5 %copy.6 = bf16[2,16,1024]{2,1,0:T(8,128)(2,1)} copy(bf16[2,16,1024]{2,1,0:T(8,128)(2,1)} %shard_map.46) | data formatting | bytes 131072

commit v3 on v2

v3 whole, which is shorter than its diff:
```python
import jax
import jax.numpy as jnp
from jax import lax
from jax.experimental import pallas as pl
from jax.experimental.pallas import tpu as pltpu
from jax.sharding import PartitionSpec as P

MESH = pl.DeviceIdType.MESH
NT = (((1,), (1,)), ((), ()))
F32 = jnp.float32
CHIPS = [(1, 0), (1, 1), (3, 0), (3, 1), (2, 0), (2, 1), (0, 1), (0, 0)]


def kernel(m_hbm, p_hbm, e_hbm, b_hbm, out_ref, mv, g, tg, acc, acc2, xbuf, part, rbuf, ex, binv, newest,
           m_sem, loc_sem, ga_s, ga_r, gt_s, gt_r, sib_s, sib_r, sh_s, sh_r, x_s, x_r, rs_s, rs_r, nb_s, nb_r, passed, pn_s, pn_r):
    lag, row = lax.axis_index("lag"), lax.axis_index("row")
    core, x, zl = lag % 2, (lag // 2) % 4, lag // 8
    y, h = row // 2, row % 2
    yp, ym, y2, ho = (y + 1) % 4, (y + 3) % 4, (y + 2) % 4, 1 - h
    W = p_hbm.shape[-1]
    S = ex.shape[1]
    older = (core == 0) & (lag > 0)

    shards = [y * 2 + h, ym * 2 + h, yp * 2 + h, y * 2 + ho, y2 * 2 + h, ym * 2 + ho, yp * 2 + ho, y2 * 2 + ho]
    sibling = lag + 1 - 2 * core
    elder = (lag + 1) % 16
    peers = [(((zl + dz) % 2) * 4 + (x + dx) % 4) for dx, dz in CHIPS]
    peer_lags = [p * 2 + core for p in peers]

    barrier = pltpu.get_barrier_semaphore()
    for k in (1, 2, 3):
        pl.semaphore_signal(barrier, 1, device_id={"row": shards[k]}, device_id_type=MESH)
    for k in range(1, 16):
        pl.semaphore_signal(barrier, 1, device_id={"lag": (lag + k) % 16}, device_id_type=MESH)

    loads = [pltpu.make_async_copy(p_hbm, g.at[row], loc_sem.at[0]),
             pltpu.make_async_copy(e_hbm.at[:, pl.ds(pl.multiple_of(lag * S, S), S)], ex, loc_sem.at[1]),
             pltpu.make_async_copy(b_hbm, binv, loc_sem.at[2])]
    m_loads = [pltpu.make_async_copy(m_hbm.at[0, :, pl.ds(pl.multiple_of(s * W, W), W)], mv.at[s], m_sem.at[k])
               for k, s in enumerate(shards)]
    for cp in loads[:1] + m_loads + loads[1:]:
        cp.start()
    loads[0].wait()
    pl.semaphore_wait(barrier, 18)

    def mm(dst, src, s, first):
        v_rows = src.shape[0] * src.shape[1]

        @pl.loop(0, 4)
        def _(n):
            cols = pl.ds(pl.multiple_of(n * (W // 4), W // 4), W // 4)
            v = lax.dot_general(src[...].reshape(v_rows, W), mv[s, cols, :], NT, preferred_element_type=F32)
            v = v.reshape(src.shape[0], src.shape[1], W // 4)
            if first:
                dst[:, :, cols] = v
            else:
                dst[:, :, cols] += v

    class Gather:
        SENDS = [(0, "0", 2), (0, "0", 1), (1, "0a", 2), (2, "0b", 1), (0, "0", 3), (1, "0", 3), (2, "0", 3), (4, "0a", 3),
                 (4, "0b", 3), (0, "1", 2), (0, "1", 1), (1, "1a", 2), (2, "1b", 1), (0, "1", 3), (3, "1", 2), (3, "1", 1),
                 (5, "1a", 2), (6, "1b", 1)]
        ARRIVE = [(1, "0"), (2, "0"), (4, "0a"), (4, "0b"), (3, "0"), (5, "0"), (6, "0"), (7, "0a"), (7, "0b"), (1, "1"),
                  (2, "1"), (4, "1a"), (4, "1b"), (3, "1"), (5, "1"), (6, "1"), (7, "1a"), (7, "1b")]

        def __init__(self, shard, total, ss, rs, split):
            self.shard, self.ss, self.rs = shard, ss, rs
            a, n = split // 2, total - split
            self.blocks = {"0": (0, split), "0a": (0, a), "0b": (a, split - a),
                           "1": (split, n), "1a": (split, n // 2), "1b": (split + n // 2, n - n // 2)}

        def copy(self, i, k, blocks, to):
            lo, n = self.blocks[blocks]
            ref = self.shard(shards[k]).at[pl.ds(lo, n)]
            return pltpu.make_async_remote_copy(ref, ref, self.ss.at[i], self.rs.at[i],
                                                device_id={"row": shards[to]}, device_id_type=MESH)

        def start(self, *which):
            for i in self.used(which):
                self.copy(i, *self.SENDS[i]).start()

        def used(self, which):
            return [i for i in which if self.blocks[self.SENDS[i][1]][1]]

        def wait(self, *which):
            for i in self.used(which):
                k, blocks = self.ARRIVE[i]
                self.copy(i, k, blocks, self.SENDS[i][2]).wait_recv()

        def drain(self):
            for i in self.used(range(18)):
                self.copy(i, *self.SENDS[i]).wait_send()

        def own(self):
            self.start(13, 0, 1, 9, 10, 4)

        def relay1(self):
            self.wait(13)
            self.start(14, 15)
            self.wait(0)
            self.start(2, 5)
            self.wait(1)
            self.start(3, 6)
            self.wait(9)
            self.start(11)
            self.wait(10)
            self.start(12)

        def relay2(self):
            self.wait(2)
            self.start(7)
            self.wait(3)
            self.start(8)
            self.wait(14)
            self.start(16)
            self.wait(15)
            self.start(17)

        def rest(self, on_shard):
            self.wait(5)
            on_shard(5)
            self.wait(6)
            on_shard(6)
            self.wait(7, 8, 16, 17)
            on_shard(7)

    def sibling_copy(k):
        ref = g.at[shards[k]]
        return pltpu.make_async_remote_copy(ref, tg.at[shards[k]], sib_s.at[k], sib_r.at[k],
                                            device_id={"lag": sibling}, device_id_type=MESH)

    shift = pltpu.make_async_remote_copy(g.at[row], tg.at[row], sh_s.at[0], sh_r.at[0],
                                         device_id={"lag": elder}, device_id_type=MESH)

    def exchange(step, k):
        return pltpu.make_async_remote_copy((acc, acc2)[step].at[peers[k] * 2 + 1 - core], xbuf.at[step, k], x_s.at[step, k],
                                            x_r.at[step, k], device_id={"lag": sibling}, device_id_type=MESH)

    def to_owner(step, k):
        return pltpu.make_async_remote_copy(part.at[step, k], rbuf.at[step, k], rs_s.at[step, k], rs_r.at[step, k],
                                            device_id={"lag": peer_lags[k]}, device_id_type=MESH)

    def reduce_send(step):
        for k in range(8):
            exchange(step, k).start()
        for k in range(8):
            exchange(step, k).wait_recv()
            part[step, k] = (acc, acc2)[step][peer_lags[k]] + xbuf[step, k]
            if k < 7:
                to_owner(step, k).start()

    def finish(step):
        history = part[step, 7]
        for k in range(7):
            to_owner(step, k).wait_recv()
            history = history + rbuf[step, k]
        source = ex[step] - history
        for b in range(binv.shape[0]):
            v = lax.dot_general(source[:, b * 128:(b + 1) * 128], binv[b], NT, precision=lax.Precision.HIGHEST,
                                preferred_element_type=F32)
            newest[step, :, pl.ds(b * 128, 128)] = v.astype(newest.dtype)
        out_ref[step] = newest[step]

    near, far = (0, 1, 2, 4), (3, 5, 6, 7)
    partner = pltpu.make_async_remote_copy(newest.at[0], passed, pn_s.at[0], pn_r.at[0],
                                           device_id={"row": shards[3]}, device_id_type=MESH)

    def to_first(k, owner=0):
        return pltpu.make_async_remote_copy(passed if owner else newest.at[0], tg.at[shards[owner], lag],
                                            nb_s.at[k + (owner > 0) * 8], nb_r.at[shards[owner]],
                                            device_id={"lag": 0, "row": shards[k]}, device_id_type=MESH)

    def to_first_own(act):
        for k in near[1:]:
            act(to_first(k))

        @pl.when(lag > 0)
        def _():
            act(to_first(0))

        @pl.when(zl == 1)
        def _():
            for k in far:
                act(to_first(k))

    def to_first_passed(act):
        @pl.when(zl == 0)
        def _():
            for k in near[1:]:
                act(to_first(k, 3))

        @pl.when((zl == 0) & (lag > 0))
        def _():
            act(to_first(0, 3))

    def first_wait(k):
        ref = tg.at[shards[k], pl.ds(1, 15)] if k in (0, 3) else tg.at[shards[k]]
        pltpu.make_async_remote_copy(ref, ref, nb_s.at[0], nb_r.at[shards[k]], device_id={"lag": 1},
                                     device_id_type=MESH).wait_recv()

    def a_shard(k):
        m_loads[k].wait()
        mm(acc, g.at[shards[k]], shards[k], k == 0)

    def t_shard(k):
        mm(acc2, tg.at[shards[k]], shards[k], k == 0)

    a = Gather(lambda s: g.at[s], 16, ga_s, ga_r, 7)
    t = Gather(lambda s: tg.at[s], 16, gt_s, gt_r, 7)

    a.own()

    @pl.when((core == 1) & (lag < 15))
    def _():
        shift.start()
    a_shard(0)
    a.relay1()
    a_shard(1)
    a.relay2()
    a_shard(2)
    a.wait(4)
    a_shard(3)
    a.wait(11, 12)
    a_shard(4)
    a.rest(a_shard)
    reduce_send(0)

    @pl.when(core == 0)
    def _():
        for k in range(8):
            sibling_copy(k).start()

    @pl.when(older)
    def _():
        shift.wait_recv()
        t.own()
    loads[1].wait()
    loads[2].wait()
    finish(0)

    @pl.when(zl == 0)
    def _():
        partner.start()
    to_first_own(lambda cp: cp.start())

    @pl.when(zl == 0)
    def _():
        partner.wait_recv()
    to_first_passed(lambda cp: cp.start())

    @pl.when(core == 1)
    def _():
        for k in range(8):
            sibling_copy(k).wait_recv()
            t_shard(k)

    @pl.when(older)
    def _():
        t_shard(0)
        t.relay1()
        t_shard(1)
        t.relay2()
        t_shard(2)
        t.wait(4)
        t_shard(3)
        t.wait(11, 12)
        t_shard(4)
        t.rest(t_shard)

    @pl.when(lag == 0)
    def _():
        tg[row, 0] = newest[0]
        tg[shards[3], 0] = passed[...]
        for n, k in enumerate(near + far):
            first_wait(k)
            mm(acc2, tg.at[shards[k]], shards[k], n == 0)

    reduce_send(1)
    finish(1)

    a.drain()
    for step in range(2):
        for k in range(8):
            exchange(step, k).wait_send()
        for k in range(7):
            to_owner(step, k).wait_send()
    to_first_own(lambda cp: cp.wait_send())
    to_first_passed(lambda cp: cp.wait_send())

    @pl.when(zl == 0)
    def _():
        partner.wait_send()

    @pl.when(older)
    def _():
        t.drain()

    @pl.when(core == 0)
    def _():
        for k in range(8):
            sibling_copy(k).wait_send()

    @pl.when((core == 1) & (lag < 15))
    def _():
        shift.wait_send()


def per_device(lag_matrix, past_current, excitation, block_inverse):
    E, W = past_current.shape[1:]
    S = E // 16
    nb = block_inverse.shape[0]
    bf = past_current.dtype
    dma = pltpu.SemaphoreType.DMA
    past = past_current.reshape(16, S, W)
    return pl.pallas_call(
        kernel,
        out_shape=jax.ShapeDtypeStruct((2, S, W), bf),
        in_specs=[pl.BlockSpec(memory_space=pl.ANY)] * 4,
        out_specs=pl.BlockSpec(memory_space=pltpu.VMEM),
        scratch_shapes=[
            pltpu.VMEM((8, W, W), bf), pltpu.VMEM((8, 16, S, W), bf), pltpu.VMEM((8, 16, S, W), bf),
            pltpu.VMEM((16, S, W), F32), pltpu.VMEM((16, S, W), F32),
            pltpu.VMEM((2, 8, S, W), F32), pltpu.VMEM((2, 8, S, W), F32), pltpu.VMEM((2, 7, S, W), F32),
            pltpu.VMEM((2, S, W), F32), pltpu.VMEM((nb, 128, 128), F32), pltpu.VMEM((2, S, W), bf),
            dma((8,)), dma((3,)), dma((18,)), dma((18,)), dma((18,)), dma((18,)), dma((8,)), dma((8,)),
            dma((1,)), dma((1,)), dma((2, 8)), dma((2, 8)), dma((2, 7)), dma((2, 7)), dma((16,)), dma((8,)),
            pltpu.VMEM((S, W), bf), dma((1,)), dma((1,)),
        ],
        compiler_params=pltpu.CompilerParams(collective_id=0, has_side_effects=True, vmem_limit_bytes=60 << 20),
    )(lag_matrix, past, excitation, block_inverse)


def solution(mesh):
    in_specs = (P("lag", "row", None), P("lag", None, "row"), P(None, None, "row"), P("row", None, None))
    return jax.shard_map(per_device, mesh=mesh, in_specs=in_specs, out_specs=P(None, "lag", "row"), check_vma=False)
```

time: 95.8 us -> 90.6 us (0.946)
  the two profiles are of different devices: /device:TPU:1 before, /device:TPU:5 now
where the time goes in v3:
time: 90.6 us; the launch traced here: 90.4 us
  Pallas kernels  88.9 us (98%)
  local copies, waits for them, and re-layouts  1.47 us (2%)
    pallas_call x1, Pallas kernels, per_device(): pl.pallas_call(kernel, out_shape=jax.ShapeDtypeStruct((2, S, W), bf), in_...  88.9 us

profile of v3, /device:TPU:5, one launch (start us, length us, event | category | flops | bytes accessed | tf_op | source)
XLA Modules:
  0.0 90.4 jit_solution(17331669381533970234)
XLA Ops:
  0.0 88.9 %shard_map.46 = bf16[2,16,1024]{2,1,0:T(8,128)(2,1)} custom-call(bf16[1,1024,8192]{2,1,0:T(8,128)(2,1)} %m_hbm.1, bf16[16,16,1024]{2,1,0:T(8,128)(2,1)} %bitcast.1, f32[2,256,1024]{2,1,0:T(8,128)} %e_hbm.1, f32[8,128,128]{2,1,0:T(8,128)} %b_hbm.1), custom_call_target="tpu_custom_call" | custom-call | tf_op jit(solution)/shard_map/pallas_call | solution.py:315
  89.0 1.5 %copy.6 = bf16[2,16,1024]{2,1,0:T(8,128)(2,1)} copy(bf16[2,16,1024]{2,1,0:T(8,128)(2,1)} %shard_map.46) | data formatting | bytes 131072

commit v4 on v3

--- a/solution.py
+++ b/solution.py
@@ -12,7 +12,7 @@
 
 
 def kernel(m_hbm, p_hbm, e_hbm, b_hbm, out_ref, mv, g, tg, acc, acc2, xbuf, part, rbuf, ex, binv, newest,
-           m_sem, loc_sem, ga_s, ga_r, gt_s, gt_r, sib_s, sib_r, sh_s, sh_r, x_s, x_r, rs_s, rs_r, nb_s, nb_r, passed, pn_s, pn_r):
+           m_sem, loc_sem, ga_s, ga_r, gt_s, gt_r, sib_s, sib_r, sh_s, sh_r, x_s, x_r, rs_s, rs_r, nb_s, nb_r, passed, pn_s, pn_r, tn, mv1, ln_s, ln_r, yb, yb_s, yb_r, b_high, b_low):
     lag, row = lax.axis_index("lag"), lax.axis_index("row")
     core, x, zl = lag % 2, (lag // 2) % 4, lag // 8
     y, h = row // 2, row % 2
@@ -43,7 +43,7 @@
     loads[0].wait()
     pl.semaphore_wait(barrier, 18)
 
-    def mm(dst, src, s, first):
+    def mm(dst, src, s, first, mv=mv):
         v_rows = src.shape[0] * src.shape[1]
 
         @pl.loop(0, 4)
@@ -155,10 +155,15 @@
             to_owner(step, k).wait_recv()
             history = history + rbuf[step, k]
         source = ex[step] - history
+        high = source.astype(newest.dtype)
+        low = (source - high.astype(F32)).astype(newest.dtype)
+        both = jnp.concatenate([high, low], axis=0)
+        S = high.shape[0]
         for b in range(binv.shape[0]):
-            v = lax.dot_general(source[:, b * 128:(b + 1) * 128], binv[b], NT, precision=lax.Precision.HIGHEST,
-                                preferred_element_type=F32)
-            newest[step, :, pl.ds(b * 128, 128)] = v.astype(newest.dtype)
+            cols = slice(b * 128, (b + 1) * 128)
+            v = lax.dot_general(both[:, cols], b_high[b], NT, preferred_element_type=F32)
+            w = lax.dot_general(high[:, cols], b_low[b], NT, preferred_element_type=F32)
+            newest[step, :, pl.ds(b * 128, 128)] = (v[:S] + (v[S:] + w)).astype(newest.dtype)
         out_ref[step] = newest[step]
 
     near, far = (0, 1, 2, 4), (3, 5, 6, 7)
@@ -166,22 +171,39 @@
                                            device_id={"row": shards[3]}, device_id_type=MESH)
 
     def to_first(k, owner=0):
-        return pltpu.make_async_remote_copy(passed if owner else newest.at[0], tg.at[shards[owner], lag],
+        where = (tg.at[row, lag] if k in near and not owner else tn.at[shards[owner] // 2, lag])
+        return pltpu.make_async_remote_copy(passed if owner else newest.at[0], where,
                                             nb_s.at[k + (owner > 0) * 8], nb_r.at[shards[owner]],
-                                            device_id={"lag": 0, "row": shards[k]}, device_id_type=MESH)
+                                            device_id={"lag": 0 if k in near and not owner else 1, "row": shards[k]},
+                                            device_id_type=MESH)
+
+    def along_y(n):
+        there = (1, 0, 2)[n]
+        return pltpu.make_async_remote_copy(newest.at[0], yb.at[there], yb_s.at[n], yb_r.at[there],
+                                            device_id={"row": shards[(1, 2, 4)[n]]}, device_id_type=MESH)
+
+    def to_first_y(n, z):
+        owner = shards[(1, 2, 4)[n]]
+        return pltpu.make_async_remote_copy(yb.at[n], tn.at[owner // 2, lag] if z else tg.at[owner, lag],
+                                            nb_s.at[8 + 4 * z + n], nb_r.at[owner],
+                                            device_id={"lag": z, "row": shards[3 * z]}, device_id_type=MESH)
 
     def to_first_own(act):
-        for k in near[1:]:
-            act(to_first(k))
-
-        @pl.when(lag > 0)
-        def _():
+        @pl.when(zl == 1)
+        def _():
+            for n in range(3):
+                act(along_y(n))
             act(to_first(0))
-
-        @pl.when(zl == 1)
-        def _():
-            for k in far:
+            act(to_first(3))
+
+        @pl.when(zl == 0)
+        def _():
+            for k in near[1:]:
                 act(to_first(k))
+
+        @pl.when((zl == 0) & (lag > 0))
+        def _():
+            act(to_first(0))
 
     def to_first_passed(act):
         @pl.when(zl == 0)
@@ -189,14 +211,27 @@
             for k in near[1:]:
                 act(to_first(k, 3))
 
-        @pl.when((zl == 0) & (lag > 0))
+        @pl.when((zl == 0) & (lag != 1))
         def _():
             act(to_first(0, 3))
 
+        @pl.when(zl == 1)
+        def _():
+            for n in range(3):
+                for z in range(2):
+                    act(to_first_y(n, z))
+
     def first_wait(k):
-        ref = tg.at[shards[k], pl.ds(1, 15)] if k in (0, 3) else tg.at[shards[k]]
-        pltpu.make_async_remote_copy(ref, ref, nb_s.at[0], nb_r.at[shards[k]], device_id={"lag": 1},
+        ref = tg.at[shards[k]] if k in near else tn.at[shards[k] // 2]
+        if k in (0, 3):
+            ref = ref.at[pl.ds(1, 15)]
+        pltpu.make_async_remote_copy(ref, ref, nb_s.at[0], nb_r.at[shards[k]], device_id={"lag": 2},
                                      device_id_type=MESH).wait_recv()
+
+    def lend(n):
+        k = far[n]
+        return pltpu.make_async_remote_copy(mv.at[shards[k]], mv1.at[shards[k] // 2], ln_s.at[n], ln_r.at[n],
+                                            device_id={"lag": 1}, device_id_type=MESH)
 
     def a_shard(k):
         m_loads[k].wait()
@@ -210,13 +245,20 @@
 
     a.own()
 
-    @pl.when((core == 1) & (lag < 15))
+    @pl.when((core == 1) & (lag < 15) & (lag != 7))
     def _():
         shift.start()
     a_shard(0)
+    loads[1].wait()
+    loads[2].wait()
+    b_high[...] = binv[...].astype(b_high.dtype)
+    b_low[...] = (binv[...] - b_high[...].astype(F32)).astype(b_low.dtype)
     a.relay1()
     a_shard(1)
     a.relay2()
+    @pl.when(lag == 7)
+    def _():
+        shift.start()
     a_shard(2)
     a.wait(4)
     a_shard(3)
@@ -230,12 +272,15 @@
         for k in range(8):
             sibling_copy(k).start()
 
+    @pl.when(lag == 0)
+    def _():
+        for n in range(4):
+            lend(n).start()
+
     @pl.when(older)
     def _():
         shift.wait_recv()
         t.own()
-    loads[1].wait()
-    loads[2].wait()
     finish(0)
 
     @pl.when(zl == 0)
@@ -246,6 +291,12 @@
     @pl.when(zl == 0)
     def _():
         partner.wait_recv()
+
+    @pl.when(zl == 1)
+    def _():
+        for n in range(3):
+            ref = yb.at[n]
+            pltpu.make_async_remote_copy(ref, ref, yb_s.at[n], yb_r.at[n], device_id={"lag": 2}, device_id_type=MESH).wait_recv()
     to_first_passed(lambda cp: cp.start())
 
     @pl.when(core == 1)
@@ -270,10 +321,17 @@
     @pl.when(lag == 0)
     def _():
         tg[row, 0] = newest[0]
-        tg[shards[3], 0] = passed[...]
-        for n, k in enumerate(near + far):
+        for n, k in enumerate(near):
             first_wait(k)
             mm(acc2, tg.at[shards[k]], shards[k], n == 0)
+
+    @pl.when(lag == 1)
+    def _():
+        tn[y, 1] = passed[...]
+        for n, k in enumerate(far):
+            lend(n).wait_recv()
+            first_wait(k)
+            mm(acc2, tn.at[shards[k] // 2], shards[k] // 2, False, mv1)
 
     reduce_send(1)
     finish(1)
@@ -290,6 +348,11 @@
     @pl.when(zl == 0)
     def _():
         partner.wait_send()
+
+    @pl.when(lag == 0)
+    def _():
+        for n in range(4):
+            lend(n).wait_send()
 
     @pl.when(older)
     def _():
@@ -324,7 +387,8 @@
             pltpu.VMEM((2, S, W), F32), pltpu.VMEM((nb, 128, 128), F32), pltpu.VMEM((2, S, W), bf),
             dma((8,)), dma((3,)), dma((18,)), dma((18,)), dma((18,)), dma((18,)), dma((8,)), dma((8,)),
             dma((1,)), dma((1,)), dma((2, 8)), dma((2, 8)), dma((2, 7)), dma((2, 7)), dma((16,)), dma((8,)),
-            pltpu.VMEM((S, W), bf), dma((1,)), dma((1,)),
+            pltpu.VMEM((S, W), bf), dma((1,)), dma((1,)), pltpu.VMEM((4, 16, S, W), bf), pltpu.VMEM((4, W, W), bf), dma((4,)), dma((4,)),
+            pltpu.VMEM((3, S, W), bf), dma((3,)), dma((3,)), pltpu.VMEM((nb, 128, 128), bf), pltpu.VMEM((nb, 128, 128), bf),
         ],
         compiler_params=pltpu.CompilerParams(collective_id=0, has_side_effects=True, vmem_limit_bytes=60 << 20),
     )(lag_matrix, past, excitation, block_inverse)

time: 90.6 us -> 89 us (0.982)
  the two profiles are of different devices: /device:TPU:5 before, /device:TPU:1 now
where the time goes in v4:
time: 89 us; the launch traced here: 88.8 us
  Pallas kernels  87.3 us (98%)
  local copies, waits for them, and re-layouts  1.47 us (2%)
    pallas_call x1, Pallas kernels, per_device(): pl.pallas_call(kernel, out_shape=jax.ShapeDtypeStruct((2, S, W), bf), in_...  87.3 us

profile of v4, /device:TPU:1, one launch (start us, length us, event | category | flops | bytes accessed | tf_op | source)
XLA Modules:
  0.0 88.8 jit_solution(2407551315560008104)
XLA Ops:
  0.0 87.3 %shard_map.46 = bf16[2,16,1024]{2,1,0:T(8,128)(2,1)} custom-call(bf16[1,1024,8192]{2,1,0:T(8,128)(2,1)} %m_hbm.1, bf16[16,16,1024]{2,1,0:T(8,128)(2,1)} %bitcast.1, f32[2,256,1024]{2,1,0:T(8,128)} %e_hbm.1, f32[8,128,128]{2,1,0:T(8,128)} %b_hbm.1), custom_call_target="tpu_custom_call" | custom-call | tf_op jit(solution)/shard_map/pallas_call | solution.py:378
  87.4 1.5 %copy.6 = bf16[2,16,1024]{2,1,0:T(8,128)(2,1)} copy(bf16[2,16,1024]{2,1,0:T(8,128)(2,1)} %shard_map.46) | data formatting | bytes 131072

commit v5 on v4

--- a/solution.py
+++ b/solution.py
@@ -240,7 +240,7 @@
     def t_shard(k):
         mm(acc2, tg.at[shards[k]], shards[k], k == 0)
 
-    a = Gather(lambda s: g.at[s], 16, ga_s, ga_r, 7)
+    a = Gather(lambda s: g.at[s], 16, ga_s, ga_r, 6)
     t = Gather(lambda s: tg.at[s], 16, gt_s, gt_r, 7)
 
     a.own()

time: 89 us -> 88.6 us (level)
  no operation moved by 1% of the time
where the time goes in v5:
time: 88.6 us; the launch traced here: 88.5 us
  Pallas kernels  87 us (98%)
  local copies, waits for them, and re-layouts  1.47 us (2%)
    pallas_call x1, Pallas kernels, per_device(): pl.pallas_call(kernel, out_shape=jax.ShapeDtypeStruct((2, S, W), bf), in_...  87 us

profile of v5, /device:TPU:1, one launch (start us, length us, event | category | flops | bytes accessed | tf_op | source)
XLA Modules:
  0.0 88.5 jit_solution(6472266849154527936)
XLA Ops:
  0.0 87.0 %shard_map.46 = bf16[2,16,1024]{2,1,0:T(8,128)(2,1)} custom-call(bf16[1,1024,8192]{2,1,0:T(8,128)(2,1)} %m_hbm.1, bf16[16,16,1024]{2,1,0:T(8,128)(2,1)} %bitcast.1, f32[2,256,1024]{2,1,0:T(8,128)} %e_hbm.1, f32[8,128,128]{2,1,0:T(8,128)} %b_hbm.1), custom_call_target="tpu_custom_call" | custom-call | tf_op jit(solution)/shard_map/pallas_call | solution.py:378
  87.0 1.5 %copy.6 = bf16[2,16,1024]{2,1,0:T(8,128)(2,1)} copy(bf16[2,16,1024]{2,1,0:T(8,128)(2,1)} %shard_map.46) | data formatting | bytes 131072

commit v6 on v5

--- a/solution.py
+++ b/solution.py
@@ -264,6 +264,10 @@
     a_shard(3)
     a.wait(11, 12)
     a_shard(4)
+    @pl.when(older & (lag != 8))
+    def _():
+        shift.wait_recv()
+        t.own()
     a.rest(a_shard)
     reduce_send(0)
 
@@ -277,7 +281,7 @@
         for n in range(4):
             lend(n).start()
 
-    @pl.when(older)
+    @pl.when(lag == 8)
     def _():
         shift.wait_recv()
         t.own()

time: 88.6 us -> 88.5 us (level)
  no operation moved by 1% of the time
where the time goes in v6:
time: 88.5 us; the launch traced here: 88.4 us
  Pallas kernels  86.9 us (98%)
  local copies, waits for them, and re-layouts  1.47 us (2%)
    pallas_call x1, Pallas kernels, per_device(): pl.pallas_call(kernel, out_shape=jax.ShapeDtypeStruct((2, S, W), bf), in_...  86.9 us

profile of v6, /device:TPU:1, one launch (start us, length us, event | category | flops | bytes accessed | tf_op | source)
XLA Modules:
  0.0 88.4 jit_solution(14538349040842150838)
XLA Ops:
  0.0 86.9 %shard_map.46 = bf16[2,16,1024]{2,1,0:T(8,128)(2,1)} custom-call(bf16[1,1024,8192]{2,1,0:T(8,128)(2,1)} %m_hbm.1, bf16[16,16,1024]{2,1,0:T(8,128)(2,1)} %bitcast.1, f32[2,256,1024]{2,1,0:T(8,128)} %e_hbm.1, f32[8,128,128]{2,1,0:T(8,128)} %b_hbm.1), custom_call_target="tpu_custom_call" | custom-call | tf_op jit(solution)/shard_map/pallas_call | solution.py:382
  86.9 1.5 %copy.6 = bf16[2,16,1024]{2,1,0:T(8,128)(2,1)} copy(bf16[2,16,1024]{2,1,0:T(8,128)(2,1)} %shard_map.46) | data formatting | bytes 131072
